TPU v7x, 32 devices: a whole 2x2x4 slice. The times are simulated.
32 devices in a mesh: grp: 2 (over x), tok: 4 (over z), head: 4 (over y, core).
Axes of the slice: x: 2, y: 2, z: 4, core: 2. Of those that a mesh axis runs over, the one named last changes fastest.
Arguments:
- views: bfloat16 [2, 2, 768, 1024], P('grp', None, 'tok'), may hold values from -6 to 6
- q_weight: bfloat16 [1024, 1024], P(None, 'head'), may hold values from -0.1875 to 0.1875
- k_weight: bfloat16 [1024, 1024], P(None, 'head'), may hold values from -0.1875 to 0.1875
- v_weight: bfloat16 [1024, 1024], P(None, 'head'), may hold values from -0.1875 to 0.1875
- rate_weight: bfloat16 [1024, 4], P(None, 'head'), may hold values from -0.1875 to 0.1875
- fast_in: float32 [4, 256, 1024], P('head', None, 'tok'), may hold values from -0.375 to 0.375
- fast_out: float32 [4, 512, 256], P('head', None, 'tok'), may hold values from -0.25 to 0.25
- out_gain: float32 [1024], P('head'), may hold values from 0.1 to 1.9
Outputs:
- rendered: bfloat16 [2, 2, 768, 1024], P('grp', None, 'tok', 'head')
All inputs are finite; a program needn't handle non-finite values.
Results may differ from a plain program's by a relative error of at most 0.013.
Values may be sent and summed in bfloat16 or wider, within the bound.
A program may use at most 64 MiB of HBM per device.

v0:
```python
import math
import jax
import jax.numpy as jnp
from jax import lax
from jax.sharding import PartitionSpec as P

norm_eps = 1e-06
out_eps = 1e-05
step_coef = 0.3
momentum_keep = 0.5


def spread(value, axis, source):
    kept = jnp.where(lax.axis_index(axis) == source, value, 0).astype(value.dtype)
    return lax.psum(kept, axis)


def rms_scale(values):
    return values * lax.rsqrt(jnp.mean(values * values, axis=-1, keepdims=True) + norm_eps)


def contract_rows(left, right):
    return lax.dot_general(
        left, right, (((0,), (0,)), ((), ())), preferred_element_type=jnp.float32
    )


def contract_cols(left, right):
    return lax.dot_general(
        left, right, (((1,), (1,)), ((), ())), preferred_element_type=jnp.float32
    )


def fast_apply(queries, copy_in, copy_out):
    hidden_units = copy_out.shape[0]
    pre_act = jnp.dot(queries, copy_in, preferred_element_type=jnp.float32)
    gate = pre_act[:, :hidden_units]
    upper = pre_act[:, hidden_units:]
    hidden = (gate * jax.nn.sigmoid(gate) * upper).astype(jnp.bfloat16)
    return jnp.dot(hidden, copy_out, preferred_element_type=jnp.float32)


def local(views, q_weight, k_weight, v_weight, rate_weight, fast_in, fast_out, out_gain):
    tok_count = lax.axis_size("tok")
    is_input = lax.axis_index("grp") == 0
    spans = views.shape[1]
    head_size = fast_in.shape[1]
    hidden_units = fast_out.shape[1]
    step_size = step_coef / math.sqrt(views.shape[2] * tok_count)
    width_all = head_size * lax.axis_size("head")
    whole_in, whole_out = (
        lax.all_gather(fast_in, "tok", axis=2, tiled=True),
        lax.all_gather(fast_out, "tok", axis=2, tiled=True),
    )
    whole_in = whole_in[0]
    whole_out = whole_out[0]
    copy_in = whole_in.astype(jnp.bfloat16)
    copy_out = whole_out.astype(jnp.bfloat16)
    state_in = fast_in[0]
    state_out = fast_out[0]
    base_in = jnp.mean(state_in * state_in, axis=0, keepdims=True)
    base_out = jnp.mean(state_out * state_out, axis=0, keepdims=True)
    moment_in = jnp.zeros_like(state_in)
    moment_out = jnp.zeros_like(state_out)

    def input_grads(inputs, given_in, given_out):
        keyed = rms_scale(jnp.dot(inputs, k_weight, preferred_element_type=jnp.float32)).astype(
            jnp.bfloat16
        )
        valued = jnp.dot(inputs, v_weight, preferred_element_type=jnp.float32)
        rates = jax.nn.softplus(jnp.dot(inputs, rate_weight, preferred_element_type=jnp.float32))
        upstream = (-(step_size * rates) * valued).astype(jnp.bfloat16)
        pre_act = jnp.dot(keyed, given_in, preferred_element_type=jnp.float32)
        gate = pre_act[:, :hidden_units]
        upper = pre_act[:, hidden_units:]
        sigma = jax.nn.sigmoid(gate)
        active = gate * sigma
        hidden = (active * upper).astype(jnp.bfloat16)
        grad_out = contract_rows(hidden, upstream)
        back = contract_cols(upstream, given_out)
        back_pre = jnp.concatenate(
            [back * upper * sigma * (1.0 + gate * (1.0 - sigma)), back * active], axis=1
        ).astype(jnp.bfloat16)
        grad_in = contract_rows(keyed, back_pre)
        return (grad_in, grad_out)

    def novel_grads(inputs, given_in, given_out):
        return (
            jnp.zeros((head_size, 2 * hidden_units), jnp.float32),
            jnp.zeros((hidden_units, head_size), jnp.float32),
        )

    outputs = []
    for span in range(spans):
        inputs = views[0, span]
        queries = rms_scale(jnp.dot(inputs, q_weight, preferred_element_type=jnp.float32)).astype(
            jnp.bfloat16
        )
        grads = lax.cond(is_input, input_grads, novel_grads, inputs, copy_in, copy_out)
        grad_in, grad_out = lax.psum_scatter(grads, "tok", scatter_dimension=1, tiled=True)
        moment_in = momentum_keep * moment_in + grad_in
        moment_out = momentum_keep * moment_out + grad_out
        trial_in = state_in - moment_in
        trial_out = state_out - moment_out
        mean_in = jnp.mean(trial_in * trial_in, axis=0, keepdims=True)
        mean_out = jnp.mean(trial_out * trial_out, axis=0, keepdims=True)
        state_in = trial_in * jnp.sqrt(base_in) * lax.rsqrt(mean_in + norm_eps)
        state_out = trial_out * jnp.sqrt(base_out) * lax.rsqrt(mean_out + norm_eps)
        part_in = state_in.astype(jnp.bfloat16)
        part_out = state_out.astype(jnp.bfloat16)
        copy_in, copy_out = (
            lax.all_gather(part_in, "tok", axis=1, tiled=True),
            lax.all_gather(part_out, "tok", axis=1, tiled=True),
        )
        copy_in, copy_out = (spread(copy_in, "grp", 0), spread(copy_out, "grp", 0))
        produced = fast_apply(queries, copy_in, copy_out)
        squares = lax.psum(jnp.sum(produced * produced, axis=1), "head")
        normed = produced * lax.rsqrt(squares / width_all + out_eps)[:, None] * out_gain
        outputs.append(normed.astype(jnp.bfloat16))
    return jnp.stack(outputs)[None]


def solution(mesh):
    placed = (
        P("grp", None, "tok", None),
        P(None, "head"),
        P(None, "head"),
        P(None, "head"),
        P(None, "head"),
        P("head", None, "tok"),
        P("head", None, "tok"),
        P("head"),
    )
    return jax.shard_map(
        local, mesh=mesh, in_specs=placed, out_specs=P("grp", None, "tok", "head"), check_vma=False
    )
```

profile of v0, /device:TPU:0, one launch (start us, length us, event | category | flops | bytes accessed | tf_op | source)
XLA Modules:
  0.0 281.3 jit_solution(5273160163596320403)
XLA Ops:
  6.5 1.2 slice_bitcast_fusion.1
  8.0 18.1 %all_gather.18 = bf16[1,512,256]{1,0,2:T(2,128)(2,1)} all-gather(bf16[1,512,64]{1,0,2:T(2,128)(2,1)S(1)} %copy.11), channel_id=1, replica_groups=mesh['grp'=2,'tok'=4,'head'=4] {'tok'}, dimensions={2}, use_global_device_ids=true | all-gather | bytes 327680 | tf_op jit(solution)/shard_map/all_gather | solution.py:53
  26.1 16.5 %all_gather.19 = bf16[1,256,1024]{2,1,0:T(8,128)(2,1)S(1)} all-gather(bf16[1,256,256]{2,1,0:T(8,128)(2,1)S(1)} %convert.16), channel_id=1, replica_groups=mesh['grp'=2,'tok'=4,'head'=4] {'tok'}, dimensions={2}, use_global_device_ids=true | all-gather | bytes 655360 | tf_op jit(solution)/shard_map/all_gather | solution.py:52
  42.6 7.0 %conditional.2 = (f32[256,1024]{1,0:T(8,128)S(1)}, f32[512,256]{1,0:T(8,128)}) conditional(s32[]{:T(128)} %convert_element_type.75, () %tuple.21, (bf16[192,1024]{1,0:T(8,128)(2,1)S(1)}, bf16[1024,256]{1,0:T(8,128)(2,1)S(1)}, bf16[1024,1]{0,1:T(2,128)(2,1)S(1)}, bf16[1024,256]{1,0:T(8,128)(2,1)S(1)}, bf16[1,512,256]{1,0,2:T(2,128)(2,1)}, ...), branch_computations={%region_1.0_spmd, %region_2.4_spmd} | conditional | flops 506758848 | bytes 14132096 | solution.py:99
  43.0 1.2 fusion.1
  44.8 0.7 copy-done.7
  46.0 1.4 multiply_convert_fusion.2
  48.6 1.1 fusion.12
  49.7 2.4 copy.18
  53.2 21.1 %reduce-scatter.13.cloned.1.call-done = f32[64,512]{1,0:T(8,128)} async-done(((f32[256,512]{1,0:T(8,128)}), f32[64,512]{1,0:T(8,128)}) %reduce-scatter.13.cloned.1.call-update) | async-done | bytes 131088
  74.3 1.0 copy.19
  75.6 15.5 %all_gather.21 = bf16[512,256]{0,1:T(8,128)(2,1)S(1)} all-gather(bf16[512,64]{0,1:T(8,128)(2,1)S(1)} %copy.14), channel_id=1, replica_groups=mesh['grp'=2,'tok'=4,'head'=4] {'tok'}, dimensions={1}, use_global_device_ids=true | all-gather | bytes 327680 | tf_op jit(solution)/shard_map/all_gather | solution.py:113
  91.9 11.3 %reduce-scatter.9.cloned.1.call-done = f32[256,256]{1,0:T(8,128)} async-done(((f32[256,1024]{1,0:T(8,128)}), f32[256,256]{1,0:T(8,128)}) %reduce-scatter.9.cloned.1.call-update) | async-done | bytes 262160 | tf_op jit(solution)/shard_map/reduce_scatter | solution.py:100
  103.2 1.1 fusion.34
  104.3 15.4 %all_gather.20 = bf16[256,1024]{1,0:T(8,128)(2,1)S(1)} all-gather(bf16[256,256]{1,0:T(8,128)(2,1)S(1)} %fusion.35), channel_id=1, replica_groups=mesh['grp'=2,'tok'=4,'head'=4] {'tok'}, dimensions={1}, use_global_device_ids=true | all-gather | bytes 655360 | tf_op jit(solution)/shard_map/all_gather | solution.py:112
  119.8 0.8 broadcast_select_fusion.1
  120.7 34.5 %all-reduce.8.cloned.1.call-done = (bf16[512,256]{0,1:T(8,128)(2,1)}, bf16[256,1024]{1,0:T(8,128)(2,1)}) async-done(((bf16[512,256]{0,1:T(8,128)(2,1)}, bf16[256,1024]{1,0:T(8,128)(2,1)}), (bf16[512,256]{0,1:T(8,128)(2,1)}, bf16[256,1024]{1,0:T(8,128)(2,1)})) %all-reduce.8.cloned.1.call-update) | async-done | bytes 786448 | tf_op jit(solution)/shard_map/psum | solution.py:15
  155.2 4.4 %conditional.3 = (f32[256,1024]{1,0:T(8,128)S(1)}, f32[512,256]{1,0:T(8,128)}) conditional(s32[]{:T(128)} %convert_element_type.75, () %tuple.23, (bf16[192,1024]{1,0:T(8,128)(2,1)S(1)}, bf16[1024,256]{1,0:T(8,128)(2,1)S(1)}, bf16[1024,1]{0,1:T(2,128)(2,1)S(1)}, bf16[1024,256]{1,0:T(8,128)(2,1)S(1)}, bf16[512,256]{0,1:T(8,128)(2,1)}, ...), branch_computations={%region_15.16_spmd, %region_16.18_spmd} | conditional | flops 506758848 | bytes 11772744 | solution.py:99
  158.4 1.1 fusion.24
  159.5 2.4 copy.20
  162.6 1.4 multiply_reduce_fusion.7
  164.4 19.5 %reduce-scatter.15.cloned.1.call-done = f32[64,512]{1,0:T(8,128)} async-done(((f32[256,512]{1,0:T(8,128)}), f32[64,512]{1,0:T(8,128)}) %reduce-scatter.15.cloned.1.call-update) | async-done | bytes 131088
  184.0 1.0 copy.21
  185.2 15.6 %all_gather.23 = bf16[512,256]{0,1:T(8,128)(2,1)S(1)} all-gather(bf16[512,64]{0,1:T(8,128)(2,1)S(1)} %copy.16), channel_id=1, replica_groups=mesh['grp'=2,'tok'=4,'head'=4] {'tok'}, dimensions={1}, use_global_device_ids=true | all-gather | bytes 327680 | tf_op jit(solution)/shard_map/all_gather | solution.py:113
  201.6 11.1 %reduce-scatter.11.cloned.1.call-done = f32[256,256]{1,0:T(8,128)} async-done(((f32[256,1024]{1,0:T(8,128)}), f32[256,256]{1,0:T(8,128)}) %reduce-scatter.11.cloned.1.call-update) | async-done | bytes 262160 | tf_op jit(solution)/shard_map/reduce_scatter | solution.py:100
  212.7 1.0 multiply_reduce_fusion.3
  213.8 15.8 %all_gather.22 = bf16[256,1024]{1,0:T(8,128)(2,1)S(1)} all-gather(bf16[256,256]{1,0:T(8,128)(2,1)S(1)} %multiply_convert_fusion.15), channel_id=1, replica_groups=mesh['grp'=2,'tok'=4,'head'=4] {'tok'}, dimensions={1}, use_global_device_ids=true | all-gather | bytes 655360 | tf_op jit(solution)/shard_map/all_gather | solution.py:112
  229.5 0.8 broadcast_select_fusion
  230.4 1.0 copy-done.8
  232.7 32.0 %all-reduce.6.cloned.1.call-done = (bf16[512,256]{0,1:T(8,128)(2,1)}, bf16[256,1024]{1,0:T(8,128)(2,1)}) async-done(((bf16[512,256]{0,1:T(8,128)(2,1)}, bf16[256,1024]{1,0:T(8,128)(2,1)}), (bf16[512,256]{0,1:T(8,128)(2,1)}, bf16[256,1024]{1,0:T(8,128)(2,1)})) %all-reduce.6.cloned.1.call-update) | async-done | bytes 786448 | tf_op jit(solution)/shard_map/psum | solution.py:15
  264.7 1.4 fusion.43
  266.5 6.4 %all-reduce = (f32[192]{0:T(256)S(1)}, f32[192]{0:T(256)S(1)}) all-reduce(f32[192]{0:T(256)S(1)} %get-tuple-element.95, f32[192]{0:T(256)S(1)} %get-tuple-element.97), channel_id=1, replica_groups=mesh['grp'=2,'tok'=4,'head'=4] {'head'}, use_global_device_ids=true, to_apply=%region_25.26 | all-reduce | flops 384 | bytes 3072 | tf_op jit(solution)/shard_map/psum | solution.py:117
  (94 shorter events, 13.2 us)
Async XLA Ops:
  6.5 156.1 %copy-start = (bf16[1024,256]{1,0:T(8,128)(2,1)S(1)}, bf16[1024,256]{1,0:T(8,128)(2,1)}, u32[]{:S(2)}) copy-start(bf16[1024,256]{1,0:T(8,128)(2,1)} %param.13) | copy-start | bytes 1572868
  6.5 67.8 %reduce-scatter.13.cloned.1.call-start = ((), (), s32[]{:S(2)}) async-start(), calls=%async_computation.6 | async-start | bytes 655360
  6.5 1.2 copy-start.12
  7.9 18.2 %copy-start.1 = (f32[1,256,256]{2,1,0:T(8,128)S(1)}, f32[1,256,256]{2,1,0:T(8,128)}, u32[]{:S(2)}) copy-start(f32[1,256,256]{2,1,0:T(8,128)} %param.17) | copy-start | bytes 786436
  7.9 34.7 %copy-start.16 = (bf16[1024,1]{0,1:T(2,128)(2,1)S(1)}, bf16[1024,1]{0,1:T(2,128)(2,1)}, u32[]{:S(2)}) copy-start(bf16[1024,1]{0,1:T(2,128)(2,1)} %param.16) | copy-start | bytes 6148
  26.1 16.5 %copy-start.5 = (bf16[1024,256]{1,0:T(8,128)(2,1)S(1)}, bf16[1024,256]{1,0:T(8,128)(2,1)}, u32[]{:S(2)}) copy-start(bf16[1024,256]{1,0:T(8,128)(2,1)} %param.14) | copy-start | bytes 1572868
  26.1 16.5 %copy-start.6 = (bf16[1024,256]{1,0:T(8,128)(2,1)S(1)}, bf16[1024,256]{1,0:T(8,128)(2,1)}, u32[]{:S(2)}) copy-start(bf16[1024,256]{1,0:T(8,128)(2,1)} %param.15) | copy-start | bytes 1572868
  44.4 1.1 copy-start.7
  44.8 1.2 copy-start.14
  47.4 1.1 copy-start.11
  47.4 1.1 copy-start.15
  49.7 2.5 copy-start.2
  52.1 51.1 %reduce-scatter.9.cloned.1.call-start = ((), (), s32[]{:S(2)}) async-start(), calls=%async_computation.4 | async-start | bytes 1310720 | tf_op jit(solution)/shard_map/reduce_scatter | solution.py:100
  52.2 0.9 copy-start.13
  52.9 102.3 %all-reduce.8.cloned.1.call-start = ((), (), s32[]{:S(2)}) async-start(), calls=%async_computation.9 | async-start | bytes 1572864 | tf_op jit(solution)/shard_map/psum | solution.py:15
  103.2 1.1 copy-start.4
  120.6 63.3 %reduce-scatter.15.cloned.1.call-start = ((), (), s32[]{:S(2)}) async-start(), calls=%async_computation.7 | async-start | bytes 655360
  155.2 1.0 copy-start.9
  156.8 1.0 copy-start.19
  159.5 2.5 copy-start.3
  162.0 50.7 %reduce-scatter.11.cloned.1.call-start = ((), (), s32[]{:S(2)}) async-start(), calls=%async_computation.5 | async-start | bytes 1310720 | tf_op jit(solution)/shard_map/reduce_scatter | solution.py:100
  162.5 1.5 copy-start.10
  162.6 102.2 %all-reduce.6.cloned.1.call-start = ((), (), s32[]{:S(2)}) async-start(), calls=%async_computation.8 | async-start | bytes 1572864 | tf_op jit(solution)/shard_map/psum | solution.py:15
  230.4 1.0 copy-start.8
  231.4 0.9 copy-start.18
  264.7 1.4 copy-start.20
  272.9 0.7 copy-start.17
Sparse Core Ops, SparseCore 0:
  52.2 22.0 reduce-scatter.12
  76.6 26.4 reduce-scatter.8
  120.7 34.3 all-reduce.7
  162.1 21.8 reduce-scatter.14
  186.1 26.5 reduce-scatter.10
  230.5 34.1 all-reduce.5
where the time goes:
time: 282 us; the launch traced here: 281 us
  waiting for transfers between devices  131 us (46%)
  blocking collectives  103 us (37%)
  local copies, waits for them, and re-layouts  14.3 us (5%)
  between operations  13.7 us (5%)
  matrix products  12.1 us (4%)
  other arithmetic  6.49 us (2%)
    psum x2, waiting for transfers between devices, spread(): return lax.psum(kept, axis)  66.5 us
    unnamed x8, waiting for transfers between devices  42 us
    all_gather x2, blocking collectives, local(): lax.all_gather(part_in, 'tok', axis=1, tiled=True)  31.2 us
    all_gather x2, blocking collectives, local(): lax.all_gather(part_out, 'tok', axis=1, tiled=True)  31.2 us
    reduce_scatter x2, waiting for transfers between devices, local(): lax.psum_scatter(grads, 'tok', scatter_dimension=1, tiled=True)  22.4 us
    all_gather x1, blocking collectives, local(): lax.all_gather(fast_out, 'tok', axis=2, tiled=True)  18.1 us
    all_gather x1, blocking collectives, local(): lax.all_gather(fast_in, 'tok', axis=2, tiled=True)  16.5 us
    unnamed x36, local copies, waits for them, and re-layouts  9.64 us
  transfers between devices with their start and end apart: 6, of which 6 were waited for; matrix products, arithmetic and copies ran while one was open for 2% of the time, Pallas kernels for 0%

commit v1 on v0

--- a/solution.py
+++ b/solution.py
@@ -8,6 +8,18 @@
 out_eps = 1e-05
 step_coef = 0.3
 momentum_keep = 0.5
+
+
+def gather_by_bits(x, axis, dim):
+    ways, here, hop = (lax.axis_size(axis), lax.axis_index(axis), x.shape[dim])
+    line, have = (x, 1)
+    while have < ways:
+        line = jnp.concatenate(
+            [line, lax.ppermute(line, axis, [(d, (d - have) % ways) for d in range(ways)])],
+            axis=dim,
+        )
+        have = 2 * have
+    return jnp.roll(line, here * hop, axis=dim)
 
 
 def spread(value, axis, source):
@@ -49,7 +61,7 @@
     step_size = step_coef / math.sqrt(views.shape[2] * tok_count)
     width_all = head_size * lax.axis_size("head")
     whole_in, whole_out = (
-        lax.all_gather(fast_in, "tok", axis=2, tiled=True),
+        gather_by_bits(fast_in, "tok", 2),
         lax.all_gather(fast_out, "tok", axis=2, tiled=True),
     )
     whole_in = whole_in[0]

time: 282 us -> 283 us (level)
  blocking collectives: 103 us -> 93.5 us
  starting transfers between devices: 0.2 us -> 6.81 us
  local copies, waits for them, and re-layouts: 14.3 us -> 18.1 us
    all_gather x1 -> x0, blocking collectives: 16.5 us -> none  [local(): lax.all_gather(fast_in, 'tok', axis=2, tiled=True)]
    ppermute x0 -> x2, starting transfers between devices: none -> 6.61 us  [gather_by_bits(): lax.ppermute(line, axis, [(d, (d - have) % ways) for d in range(ways)])]
    all_gather x1, blocking collectives: 18.1 us -> 24.3 us  [local(): lax.all_gather(fast_out, 'tok', axis=2, tiled=True)]
    unnamed x36 -> x46, local copies, waits for them, and re-layouts: 9.64 us -> 13 us
  transfers between devices with their start and end apart: 6 -> 8, of which waited for: 6 -> 7; matrix products, arithmetic and copies ran while one was open for 2% -> 3% of each run, Pallas kernels for 0% -> 0%
where the time goes in v1:
time: 283 us
  waiting for transfers between devices  130 us (46%)
  blocking collectives  93.5 us (33%)
  local copies, waits for them, and re-layouts  18.1 us (6%)
  between operations  13.7 us (5%)
  matrix products  12.3 us (4%)
  other arithmetic  8.43 us (3%)
  starting transfers between devices  6.81 us (2%)
    psum x2, waiting for transfers between devices, spread(): return lax.psum(kept, axis)  65.1 us
    unnamed x8, waiting for transfers between devices  39.6 us
    all_gather x2, blocking collectives, local(): lax.all_gather(part_in, 'tok', axis=1, tiled=True)  31.7 us
    all_gather x2, blocking collectives, local(): lax.all_gather(part_out, 'tok', axis=1, tiled=True)  31.1 us
    all_gather x1, blocking collectives, local(): lax.all_gather(fast_out, 'tok', axis=2, tiled=True)  24.3 us
    reduce_scatter x2, waiting for transfers between devices, local(): lax.psum_scatter(grads, 'tok', scatter_dimension=1, tiled=True)  22.2 us
    unnamed x46, local copies, waits for them, and re-layouts  13 us
    ppermute x2, starting transfers between devices, gather_by_bits(): lax.ppermute(line, axis, [(d, (d - have) % ways) for d in range(ways)])  6.61 us
  transfers between devices with their start and end apart: 8, of which 7 were waited for; matrix products, arithmetic and copies ran while one was open for 3% of the time, Pallas kernels for 0%

profile of v1, /device:TPU:0, one launch (start us, length us, event | category | flops | bytes accessed | tf_op | source)
XLA Modules:
  0.0 282.7 jit_solution(2551020210425110188)
XLA Ops:
  6.5 1.8 fusion.52
  8.4 5.1 %collective-permute-start = (bf16[1,256,256]{2,1,0:T(8,128)(2,1)S(1)}, bf16[1,256,256]{2,1,0:T(8,128)(2,1)S(1)}, u32[]{:S(2)}, u32[]{:S(2)}) collective-permute-start(bf16[1,256,256]{2,1,0:T(8,128)(2,1)S(1)} %get-tuple-element.220), channel_id=1, source_target_pairs={{0,12},{4,0},{8,4},{12,8},{1,13},{5,1},{9,5},{13,9},{2,14},{6,2},{... | collective-permute-start | bytes 393224 | tf_op jit(solution)/shard_map/ppermute | solution.py:18
  13.5 2.8 collective-permute-done
  16.3 1.5 collective-permute-start.1
  18.0 24.3 %all_gather.15 = bf16[1,512,256]{1,0,2:T(2,128)(2,1)} all-gather(bf16[1,512,64]{1,0,2:T(2,128)(2,1)S(1)} %copy.11), channel_id=1, replica_groups=mesh['grp'=2,'tok'=4,'head'=4] {'tok'}, dimensions={2}, use_global_device_ids=true | all-gather | bytes 327680 | tf_op jit(solution)/shard_map/all_gather | solution.py:65
  45.9 8.0 %conditional.2 = (f32[256,1024]{1,0:T(8,128)S(1)}, f32[512,256]{1,0:T(8,128)}) conditional(s32[]{:T(128)} %convert_element_type.93, () %tuple.32, (bf16[192,1024]{1,0:T(8,128)(2,1)S(1)}, bf16[1024,256]{1,0:T(8,128)(2,1)S(1)}, bf16[1024,1]{0,1:T(2,128)(2,1)S(1)}, bf16[1024,256]{1,0:T(8,128)(2,1)S(1)}, bf16[1,512,256]{1,0,2:T(2,128)(2,1)}, ...), branch_computations={%region_1.2_spmd, %region_2.4_spmd.clone} | conditional | flops 506758848 | bytes 18326844 | solution.py:111
  47.2 1.3 fusion.15
  50.2 1.4 multiply_convert_fusion.9
  52.8 1.1 fusion.25
  53.9 2.4 copy.18
  57.5 18.8 %reduce-scatter.13.cloned.1.call-done = f32[64,512]{1,0:T(8,128)} async-done(((f32[256,512]{1,0:T(8,128)}), f32[64,512]{1,0:T(8,128)}) %reduce-scatter.13.cloned.1.call-update) | async-done | bytes 131088
  76.3 1.0 copy.19
  78.1 15.5 %all_gather.17 = bf16[512,256]{0,1:T(8,128)(2,1)S(1)} all-gather(bf16[512,64]{0,1:T(8,128)(2,1)S(1)} %copy.14), channel_id=1, replica_groups=mesh['grp'=2,'tok'=4,'head'=4] {'tok'}, dimensions={1}, use_global_device_ids=true | all-gather | bytes 327680 | tf_op jit(solution)/shard_map/all_gather | solution.py:125
  94.4 11.0 %reduce-scatter.9.cloned.1.call-done = f32[256,256]{1,0:T(8,128)} async-done(((f32[256,1024]{1,0:T(8,128)}), f32[256,256]{1,0:T(8,128)}) %reduce-scatter.9.cloned.1.call-update) | async-done | bytes 262160 | tf_op jit(solution)/shard_map/reduce_scatter | solution.py:112
  105.4 1.1 fusion.35
  106.6 15.9 %all_gather.16 = bf16[256,1024]{1,0:T(8,128)(2,1)S(1)} all-gather(bf16[256,256]{1,0:T(8,128)(2,1)S(1)} %fusion.36), channel_id=1, replica_groups=mesh['grp'=2,'tok'=4,'head'=4] {'tok'}, dimensions={1}, use_global_device_ids=true | all-gather | bytes 655360 | tf_op jit(solution)/shard_map/all_gather | solution.py:124
  122.5 0.8 broadcast_select_fusion.1
  123.4 33.3 %all-reduce.8.cloned.1.call-done = (bf16[512,256]{0,1:T(8,128)(2,1)}, bf16[256,1024]{1,0:T(8,128)(2,1)}) async-done(((bf16[512,256]{0,1:T(8,128)(2,1)}, bf16[256,1024]{1,0:T(8,128)(2,1)}), (bf16[512,256]{0,1:T(8,128)(2,1)}, bf16[256,1024]{1,0:T(8,128)(2,1)})) %all-reduce.8.cloned.1.call-update) | async-done | bytes 786448 | tf_op jit(solution)/shard_map/psum | solution.py:27
  156.7 4.4 %conditional.3 = (f32[256,1024]{1,0:T(8,128)S(1)}, f32[512,256]{1,0:T(8,128)}) conditional(s32[]{:T(128)} %convert_element_type.93, () %tuple.34, (bf16[192,1024]{1,0:T(8,128)(2,1)S(1)}, bf16[1024,256]{1,0:T(8,128)(2,1)S(1)}, bf16[1024,1]{0,1:T(2,128)(2,1)S(1)}, bf16[1024,256]{1,0:T(8,128)(2,1)S(1)}, bf16[512,256]{0,1:T(8,128)(2,1)}, ...), branch_computations={%region_15.16_spmd, %region_16.18_spmd} | conditional | flops 506758848 | bytes 11772744 | solution.py:111
  160.0 1.1 fusion.6
  161.1 2.4 copy.20
  164.2 1.4 multiply_reduce_fusion.7
  166.0 19.5 %reduce-scatter.15.cloned.1.call-done = f32[64,512]{1,0:T(8,128)} async-done(((f32[256,512]{1,0:T(8,128)}), f32[64,512]{1,0:T(8,128)}) %reduce-scatter.15.cloned.1.call-update) | async-done | bytes 131088
  185.5 1.0 copy.21
  186.8 15.5 %all_gather.19 = bf16[512,256]{0,1:T(8,128)(2,1)S(1)} all-gather(bf16[512,64]{0,1:T(8,128)(2,1)S(1)} %copy.16), channel_id=1, replica_groups=mesh['grp'=2,'tok'=4,'head'=4] {'tok'}, dimensions={1}, use_global_device_ids=true | all-gather | bytes 327680 | tf_op jit(solution)/shard_map/all_gather | solution.py:125
  203.1 11.2 %reduce-scatter.11.cloned.1.call-done = f32[256,256]{1,0:T(8,128)} async-done(((f32[256,1024]{1,0:T(8,128)}), f32[256,256]{1,0:T(8,128)}) %reduce-scatter.11.cloned.1.call-update) | async-done | bytes 262160 | tf_op jit(solution)/shard_map/reduce_scatter | solution.py:112
  214.3 1.0 multiply_reduce_fusion.3
  215.4 15.8 %all_gather.18 = bf16[256,1024]{1,0:T(8,128)(2,1)S(1)} all-gather(bf16[256,256]{1,0:T(8,128)(2,1)S(1)} %multiply_convert_fusion.15), channel_id=1, replica_groups=mesh['grp'=2,'tok'=4,'head'=4] {'tok'}, dimensions={1}, use_global_device_ids=true | all-gather | bytes 655360 | tf_op jit(solution)/shard_map/all_gather | solution.py:124
  232.0 1.0 copy-done.8
  234.3 31.8 %all-reduce.6.cloned.1.call-done = (bf16[512,256]{0,1:T(8,128)(2,1)}, bf16[256,1024]{1,0:T(8,128)(2,1)}) async-done(((bf16[512,256]{0,1:T(8,128)(2,1)}, bf16[256,1024]{1,0:T(8,128)(2,1)}), (bf16[512,256]{0,1:T(8,128)(2,1)}, bf16[256,1024]{1,0:T(8,128)(2,1)})) %all-reduce.6.cloned.1.call-update) | async-done | bytes 786448 | tf_op jit(solution)/shard_map/psum | solution.py:27
  266.1 1.4 fusion.44
  267.9 6.4 %all-reduce = (f32[192]{0:T(256)S(1)}, f32[192]{0:T(256)S(1)}) all-reduce(f32[192]{0:T(256)S(1)} %get-tuple-element.228, f32[192]{0:T(256)S(1)} %get-tuple-element.230), channel_id=1, replica_groups=mesh['grp'=2,'tok'=4,'head'=4] {'head'}, use_global_device_ids=true, to_apply=%region_25.26 | all-reduce | flops 384 | bytes 3072 | tf_op jit(solution)/shard_map/psum | solution.py:129
  (111 shorter events, 19.8 us)
Async XLA Ops:
  6.5 157.6 %copy-start = (bf16[1024,256]{1,0:T(8,128)(2,1)S(1)}, bf16[1024,256]{1,0:T(8,128)(2,1)}, u32[]{:S(2)}) copy-start(bf16[1024,256]{1,0:T(8,128)(2,1)} %param.13) | copy-start | bytes 1572868
  6.5 9.7 %copy-start.1 = (f32[1,256,256]{2,1,0:T(8,128)S(1)}, f32[1,256,256]{2,1,0:T(8,128)}, u32[]{:S(2)}) copy-start(f32[1,256,256]{2,1,0:T(8,128)} %param.17) | copy-start | bytes 786436
  6.5 11.3 %copy-start.10 = (bf16[1,2,192,1024]{3,2,1,0:T(8,128)(2,1)S(1)}, bf16[1,2,192,1024]{3,2,1,0:T(8,128)(2,1)}, u32[]{:S(2)}) copy-start(bf16[1,2,192,1024]{3,2,1,0:T(8,128)(2,1)} %param.12) | copy-start | bytes 2359300
  6.5 69.7 %reduce-scatter.13.cloned.1.call-start = ((), (), s32[]{:S(2)}) async-start(), calls=%async_computation.6 | async-start | bytes 655360
  8.4 7.8 %collective-permute-start = (bf16[1,256,256]{2,1,0:T(8,128)(2,1)S(1)}, bf16[1,256,256]{2,1,0:T(8,128)(2,1)S(1)}, u32[]{:S(2)}, u32[]{:S(2)}) collective-permute-start(bf16[1,256,256]{2,1,0:T(8,128)(2,1)S(1)} %get-tuple-element.220), channel_id=1, source_target_pairs={{0,12},{4,0},{8,4},{12,8},{1,13},{5,1},{9,5},{13,9},{2,14},{6,2},{... | collective-permute-start | bytes 393224 | tf_op jit(solution)/shard_map/ppermute | solution.py:18
  16.3 1.6 copy-start.14
  16.3 26.7 %collective-permute-start.1 = (bf16[1,256,512]{2,1,0:T(8,128)(2,1)S(1)}, bf16[1,256,512]{2,1,0:T(8,128)(2,1)S(1)}, u32[]{:S(2)}, u32[]{:S(2)}) collective-permute-start(bf16[1,256,512]{2,1,0:T(8,128)(2,1)S(1)} %pad_maximum_fusion), channel_id=1, source_target_pairs={{0,8},{4,12},{8,0},{12,4},{1,9},{5,13},{9,1},{13,5},{2,10},{6,14},... | collective-permute-start | bytes 786440 | tf_op jit(solution)/shard_map/ppermute | solution.py:18
  43.8 2.1 copy-start.6
  44.5 1.4 copy-start.5
  45.2 0.7 copy-start.18
  45.9 1.2 copy-start.13
  48.7 1.0 copy-start.7
  49.0 1.2 copy-start.16
  51.7 1.1 copy-start.12
  51.7 1.1 copy-start.17
  53.9 2.5 copy-start.2
  56.4 49.0 %reduce-scatter.9.cloned.1.call-start = ((), (), s32[]{:S(2)}) async-start(), calls=%async_computation.4 | async-start | bytes 1310720 | tf_op jit(solution)/shard_map/reduce_scatter | solution.py:112
  56.4 0.9 copy-start.15
  57.1 99.6 %all-reduce.8.cloned.1.call-start = ((), (), s32[]{:S(2)}) async-start(), calls=%async_computation.9 | async-start | bytes 1572864 | tf_op jit(solution)/shard_map/psum | solution.py:27
  105.4 1.1 copy-start.4
  123.4 62.1 %reduce-scatter.15.cloned.1.call-start = ((), (), s32[]{:S(2)}) async-start(), calls=%async_computation.7 | async-start | bytes 655360
  156.7 1.0 copy-start.9
  158.3 1.0 copy-start.23
  161.1 2.5 copy-start.3
  163.5 50.8 %reduce-scatter.11.cloned.1.call-start = ((), (), s32[]{:S(2)}) async-start(), calls=%async_computation.5 | async-start | bytes 1310720 | tf_op jit(solution)/shard_map/reduce_scatter | solution.py:112
  164.1 1.5 copy-start.11
  164.1 102.0 %all-reduce.6.cloned.1.call-start = ((), (), s32[]{:S(2)}) async-start(), calls=%async_computation.8 | async-start | bytes 1572864 | tf_op jit(solution)/shard_map/psum | solution.py:27
  185.5 1.1 copy-start.20
  232.0 1.0 copy-start.8
  233.0 0.9 copy-start.22
  266.1 1.4 copy-start.24
  274.3 0.7 copy-start.21
  (1 other events, 0.5 us)
Sparse Core Ops, SparseCore 0:
  56.5 19.7 reduce-scatter.12
  78.6 26.7 reduce-scatter.8
  123.5 33.1 all-reduce.7
  163.6 21.8 reduce-scatter.14
  187.6 26.6 reduce-scatter.10
  232.1 33.9 all-reduce.5
